TPU v7x, 512 devices: a whole 4x8x8 slice. The times are simulated.
512 devices in a mesh: dp: 32 (over z, y_hi), tensor: 16 (over x, y_lo, core).
Axes of the slice: x: 4, y: 8 (y_hi: 4, y_lo: 2; y = y_hi * 2 + y_lo), z: 8, core: 2. Of those that a mesh axis runs over, the one named last changes fastest.
Arguments:
- hidden: bfloat16 [16384, 7168], P('dp', 'tensor'), may hold values from -6 to 6
- w_down: bfloat16 [7168, 576], P('tensor'), may hold values from -0.0625 to 0.0625
- norm_gain: float32 [512], replicated, may hold values from 0.25 to 1.75
- w_up: bfloat16 [512, 32768], P('dp', 'tensor'), may hold values from -0.25 to 0.25
- kv_grad: bfloat16 [16384, 32768], P('dp', 'tensor'), may hold values from -6 to 6
- rope_grad: bfloat16 [16384, 64], P('dp'), may hold values from -6 to 6
Outputs:
- hidden_grad: bfloat16 [16384, 7168], P('dp', 'tensor')
- down_grad: bfloat16 [7168, 576], P('tensor')
- gain_grad: float32 [512], replicated
- up_grad: bfloat16 [512, 32768], P('dp', 'tensor')
All inputs are finite; a program needn't handle non-finite values.
Results may differ from a plain program's by a relative error of at most 0.005.
Values may be sent and summed in bfloat16 or wider, within the bound.
No kernel may reach another device: no remote copies, remote signals or barrier semaphores. Data moves between devices by JAX's collectives and lax.ppermute only.
A program may use at most 64 MiB of HBM per device.

v0:
```python
import jax
import jax.numpy as jnp
from jax import lax
from jax.sharding import Mesh
from jax.sharding import PartitionSpec as P

ALL = ("z", "yh", "x", "yl", "core")
DP = ("z", "yh")
TENSOR = ("x", "yl", "core")
GAIN_ROWS = 8
LANES = 512


def dot(a, b, dims):
    return lax.dot_general(a, b, (dims, ((), ())), preferred_element_type=jnp.float32)


def two_halves(value):
    high = value.astype(jnp.bfloat16)
    low = (value - high.astype(jnp.float32)).astype(jnp.bfloat16)
    return (high, low)


def scatter_sum(partial, axes, parts):
    pieces = partial.reshape((parts, -1) + partial.shape[1:])
    arrived = lax.all_to_all(pieces, axes, 0, 0, tiled=True)
    return jnp.sum(arrived.astype(jnp.float32), axis=0)


def spread(piece, axes, parts):
    copies = jnp.broadcast_to(piece[None], (parts,) + piece.shape)
    return lax.all_to_all(copies, axes, 0, 0, tiled=True)


def after(value, earlier):
    return lax.optimization_barrier((value, earlier))[0]


def with_gain(down, gain):
    high, low = two_halves(gain)
    lanes = jnp.stack([high, low], axis=-2)
    rows = [(0, 0)] * (lanes.ndim - 2) + [(0, down.shape[-2] - 2), (0, 0)]
    return jnp.concatenate([down.astype(jnp.bfloat16), jnp.pad(lanes, rows)], axis=-1)


def parted(both, width):
    lanes = both[..., :2, width:].astype(jnp.float32)
    return (both[..., :width], lanes[..., 0, :] + lanes[..., 1, :])


def body(sizes, hidden, w_down, norm_gain, w_up, kv_grad, rope_grad):
    n_z, n_yh, n_t = sizes
    lat = norm_gain.shape[0]
    width = w_down.shape[1]
    w_up_near = spread(w_up, "yh", n_yh).reshape(-1, w_up.shape[1])
    w_up_all = lax.all_gather(w_up_near, "z", axis=0, tiled=True)
    projected = scatter_sum(dot(hidden, w_down[:, :lat], ((1,), (0,))), TENSOR, n_t)
    inv_rms = lax.rsqrt(jnp.mean(projected * projected, axis=1, keepdims=True) + 1e-06)
    latent = (projected * inv_rms * norm_gain).astype(jnp.bfloat16)
    latent_all = spread(latent, TENSOR, n_t).reshape(-1, lat)
    up_part = dot(latent_all, kv_grad, ((0,), (0,))).astype(jnp.bfloat16)
    up_sum = lax.psum_scatter(up_part, "z", scatter_dimension=0, tiled=True)
    grad_part = dot(kv_grad, after(w_up_all, up_part), ((1,), (1,)))
    latent_grad = scatter_sum(grad_part.astype(jnp.bfloat16), TENSOR, n_t)
    gain_share = jnp.sum(latent_grad * projected * inv_rms, axis=0)
    scaled = norm_gain * latent_grad
    proj_grad = (
        inv_rms * scaled
        - projected
        * inv_rms
        * inv_rms
        * inv_rms
        * jnp.sum(scaled * projected, axis=1, keepdims=True)
        / lat
    ).astype(jnp.bfloat16)
    high, low = two_halves(gain_share)
    fill = jnp.zeros((GAIN_ROWS - 2, lat), jnp.bfloat16)
    joined = spread(jnp.concatenate([proj_grad, high[None], low[None], fill], axis=0), TENSOR, n_t)
    rows = proj_grad.shape[0]
    joint_grad = jnp.concatenate([joined[:, :rows].reshape(-1, lat), rope_grad], axis=1)
    gain_group = jnp.sum(joined[:, rows : rows + 2].astype(jnp.float32), axis=(0, 1))
    hidden_grad = dot(joint_grad, w_down, ((1,), (1,))).astype(jnp.bfloat16)
    down_part = dot(hidden, joint_grad, ((0,), (0,)))
    packed = with_gain(down_part.reshape(n_z, -1, width), gain_group.reshape(n_z, -1))
    arrived = lax.all_to_all(packed, "z", 0, 0, tiled=True).astype(jnp.float32)
    down_sum, gain_sum = parted(jnp.sum(arrived, axis=0), width)
    packed = with_gain(down_sum, gain_sum)
    near = packed.shape[0]
    up_rows = up_sum.shape[0] // n_yh
    up_cut = up_sum.reshape(n_yh, up_rows, -1, LANES).transpose(0, 2, 1, 3)
    up_cut = up_cut.reshape(n_yh, -1, LANES)
    up_cut = jnp.pad(up_cut, [(0, 0), (0, 0), (0, packed.shape[1] - LANES)])
    copies = jnp.broadcast_to(packed[None], (n_yh,) + packed.shape)
    both = jnp.concatenate([copies, up_cut], axis=1)
    arrived = lax.all_to_all(both, "yh", 0, 0, tiled=True)
    up_grad = jnp.sum(arrived[:, near:, :LANES].astype(jnp.float32), axis=0)
    up_grad = up_grad.reshape(-1, up_rows, LANES).transpose(1, 0, 2)
    up_grad = up_grad.reshape(up_rows, -1).astype(jnp.bfloat16)
    down_sum, gain_sum = parted(jnp.sum(arrived[:, :near].astype(jnp.float32), axis=0), width)
    arrived = spread(with_gain(down_sum, gain_sum), "z", n_z)
    down_grad, gain_grad = parted(arrived, width)
    return (hidden_grad, down_grad.reshape(-1, width), gain_grad.reshape(-1), up_grad)


def solution(mesh):
    n_z, n_yh, n_x, n_yl, n_core = (8, 4, 4, 2, 2)
    fine = Mesh(mesh.devices.reshape(n_z, n_yh, n_x, n_yl, n_core), ALL)

    def shards(*args):
        return body((n_z, n_yh, n_x * n_yl * n_core), *args)

    return jax.shard_map(
        shards,
        mesh=fine,
        in_specs=(P(DP, TENSOR), P(TENSOR, None), P(), P(DP, TENSOR), P(DP, TENSOR), P(DP, None)),
        out_specs=(P(DP, TENSOR), P(TENSOR, None), P(), P(DP, TENSOR)),
        check_vma=False,
    )
```

profile of v0, /device:TPU:23, one launch (start us, length us, event | category | flops | bytes accessed | tf_op | source)
XLA Modules:
  0.0 202.4 jit_solution(13560294213130005437)
XLA Ops:
  7.2 1.7 broadcast_in_dim.12
  8.9 6.9 %all-to-all-start.1 = ((bf16[4,16,2048]{2,1,0:T(8,128)(2,1)}), bf16[4,16,2048]{2,1,0:T(8,128)(2,1)S(1)}, u32[]{:S(2)}, u32[]{:S(2)}) async-start(bf16[4,16,2048]{2,1,0:T(8,128)(2,1)} %broadcast_in_dim.12), calls=%async_computation.1 | async-start | bytes 524288 | tf_op jit(solution)/shard_map/all_to_all | solution.py:32
  15.8 2.6 %fusion.2 = f32[512,512]{1,0:T(8,128)} fusion(bf16[512,448]{0,1:T(8,128)(2,1)} %param.6, bf16[448,576]{1,0:T(8,128)(2,1)} %param.7), kind=kOutput, calls=%fused_computation.12 | convolution fusion | flops 234881024 | bytes 1966080 | tf_op jit(solution)/shard_map/dot_general | solution.py:15
  18.4 7.4 %all-to-all-done.1 = bf16[4,16,2048]{2,1,0:T(8,128)(2,1)S(1)} async-done(((bf16[4,16,2048]{2,1,0:T(8,128)(2,1)}), bf16[4,16,2048]{2,1,0:T(8,128)(2,1)S(1)}, u32[]{:S(2)}, u32[]{:S(2)}) %all-to-all-start.1) | async-done | bytes 262176 | tf_op jit(solution)/shard_map/all_to_all | solution.py:32
  25.8 5.3 %all-to-all-start = ((f32[16,32,512]{2,1,0:T(8,128)}), f32[16,32,512]{2,1,0:T(8,128)S(1)}, u32[]{:S(2)}, u32[]{:S(2)}) async-start(f32[16,32,512]{2,1,0:T(8,128)} %bitcast.28), calls=%async_computation | async-start | bytes 2097152 | tf_op jit(solution)/shard_map/all_to_all | solution.py:26
  31.8 13.0 %all-to-all-done = f32[16,32,512]{2,1,0:T(8,128)S(1)} async-done(((f32[16,32,512]{2,1,0:T(8,128)}), f32[16,32,512]{2,1,0:T(8,128)S(1)}, u32[]{:S(2)}, u32[]{:S(2)}) %all-to-all-start) | async-done | bytes 1048608 | tf_op jit(solution)/shard_map/all_to_all | solution.py:26
  45.2 13.3 %all_to_all.40 = bf16[16,32,512]{2,1,0:T(8,128)(2,1)S(1)} all-to-all(bf16[16,32,512]{2,1,0:T(8,128)(2,1)S(1)} %broadcast_in_dim.13), channel_id=1, replica_groups=mesh['z'=8,'yh'=4,'x'=4,'yl'=2,'core'=2] {'x','yl','core'}, dimensions={0} | all-to-all | bytes 1048576 | tf_op jit(solution)/shard_map/all_to_all | solution.py:32
  58.4 2.6 %convolution_convert_fusion = bf16[512,2048]{1,0:T(8,128)(2,1)} fusion(bf16[512,512]{1,0:T(8,128)(2,1)S(1)} %bitcast.35, bf16[512,2048]{1,0:T(8,128)(2,1)S(1)} %copy-done), kind=kOutput, calls=%fused_computation | convolution fusion | flops 1074790400 | bytes 4718592 | tf_op jit(solution)/shard_map/dot_general | solution.py:15
  61.1 15.9 %all-gather.2.cloned.1.call-done = bf16[512,2048]{1,0:T(8,128)(2,1)} async-done(((bf16[64,2048]{1,0:T(8,128)(2,1)}), bf16[512,2048]{1,0:T(8,128)(2,1)}) %all-gather.2.cloned.1.call-update) | async-done | bytes 2097168 | tf_op jit(solution)/shard_map/all_gather | solution.py:56
  77.0 3.7 %convolution_convert_fusion.2 = bf16[512,512]{0,1:T(8,128)(2,1)} fusion(bf16[512,2048]{1,0:T(8,128)(2,1)} %all-gather.2.cloned.1.call-done, bf16[512,2048]{1,0:T(8,128)(2,1)S(1)} %copy-done), kind=kOutput, calls=%fused_computation.2 | convolution fusion | flops 1074003968 | bytes 4718592 | tf_op jit(solution)/shard_map/dot_general | solution.py:15
  80.6 10.1 %all-to-all-start.3 = ((bf16[16,32,512]{2,1,0:T(8,128)(2,1)}), bf16[16,32,512]{2,1,0:T(8,128)(2,1)S(1)}, u32[]{:S(2)}, u32[]{:S(2)}) async-start(bf16[16,32,512]{2,1,0:T(8,128)(2,1)} %bitcast.4), calls=%async_computation.3 | async-start | bytes 1048576 | tf_op jit(solution)/shard_map/all_to_all | solution.py:26
  91.6 6.9 %all-to-all-done.3 = bf16[16,32,512]{2,1,0:T(8,128)(2,1)S(1)} async-done(((bf16[16,32,512]{2,1,0:T(8,128)(2,1)}), bf16[16,32,512]{2,1,0:T(8,128)(2,1)S(1)}, u32[]{:S(2)}, u32[]{:S(2)}) %all-to-all-start.3) | async-done | bytes 524320 | tf_op jit(solution)/shard_map/all_to_all | solution.py:26
  98.9 0.9 broadcast_in_dim.15
  99.8 6.8 %all-to-all-start.4 = ((bf16[16,40,512]{2,1,0:T(8,128)(2,1)}), bf16[16,40,512]{2,1,0:T(8,128)(2,1)S(1)}, u32[]{:S(2)}, u32[]{:S(2)}) async-start(bf16[16,40,512]{2,1,0:T(8,128)(2,1)} %broadcast_in_dim.15), calls=%async_computation.4 | async-start | bytes 1310720 | tf_op jit(solution)/shard_map/all_to_all | solution.py:32
  106.7 9.4 %all-to-all-done.4 = bf16[16,40,512]{2,1,0:T(8,128)(2,1)S(1)} async-done(((bf16[16,40,512]{2,1,0:T(8,128)(2,1)}), bf16[16,40,512]{2,1,0:T(8,128)(2,1)S(1)}, u32[]{:S(2)}, u32[]{:S(2)}) %all-to-all-start.4) | async-done | bytes 655392 | tf_op jit(solution)/shard_map/all_to_all | solution.py:32
  117.7 0.9 pad_maximum_fusion.1
  118.6 3.9 %all-to-all-start.5 = ((bf16[8,56,640]{2,1,0:T(8,128)(2,1)}), bf16[8,56,640]{2,1,0:T(8,128)(2,1)S(1)}, u32[]{:S(2)}, u32[]{:S(2)}) async-start(bf16[8,56,640]{2,1,0:T(8,128)(2,1)} %pad_maximum_fusion.1), calls=%async_computation.5 | async-start | bytes 1146880 | tf_op jit(solution)/shard_map/all_to_all | solution.py:85
  122.5 18.2 %reduce-scatter.2.cloned.1.call-done = bf16[64,2048]{1,0:T(8,128)(2,1)} async-done(((bf16[512,2048]{1,0:T(8,128)(2,1)}), bf16[64,2048]{1,0:T(8,128)(2,1)}) %reduce-scatter.2.cloned.1.call-update) | async-done | bytes 262160 | tf_op jit(solution)/shard_map/reduce_scatter | solution.py:62
  140.6 1.1 reshape.144
  141.8 3.1 %all-to-all-done.5 = bf16[8,56,640]{2,1,0:T(8,128)(2,1)S(1)} async-done(((bf16[8,56,640]{2,1,0:T(8,128)(2,1)}), bf16[8,56,640]{2,1,0:T(8,128)(2,1)S(1)}, u32[]{:S(2)}, u32[]{:S(2)}) %all-to-all-start.5) | async-done | bytes 573472 | tf_op jit(solution)/shard_map/all_to_all | solution.py:85
  145.3 17.1 %all_to_all.41 = bf16[4,120,640]{2,1,0:T(8,128)(2,1)S(1)} all-to-all(bf16[4,120,640]{2,1,0:T(8,128)(2,1)S(1)} %fusion.1), channel_id=1, replica_groups=mesh['z'=8,'yh'=4,'x'=4,'yl'=2,'core'=2] {'yh'}, dimensions={0} | all-to-all | bytes 1228800 | tf_op jit(solution)/shard_map/all_to_all | solution.py:95
  163.4 11.6 %all-to-all-start.7 = ((bf16[8,56,640]{2,1,0:T(8,128)(2,1)}), bf16[8,56,640]{2,1,0:T(8,128)(2,1)S(1)}, u32[]{:S(2)}, u32[]{:S(2)}) async-start(bf16[8,56,640]{2,1,0:T(8,128)(2,1)} %broadcast_in_dim.17), calls=%async_computation.8 | async-start | bytes 1146880 | tf_op jit(solution)/shard_map/all_to_all | solution.py:32
  175.0 2.5 %convolution_convert_fusion.3 = bf16[512,448]{0,1:T(8,128)(2,1)} fusion(bf16[448,576]{1,0:T(8,128)(2,1)} %param.7, bf16[512,64]{1,0:T(8,128)(2,1)S(1)} %copy.27, bf16[512,512]{1,0:T(8,128)(2,1)} %bitcast.34), kind=kOutput, calls=%fused_computation.3 | convolution fusion | flops 265650176 | bytes 1564672 | tf_op jit(solution)/shard_map/dot_general | solution.py:15
  178.2 15.8 %all-to-all-done.7 = bf16[8,56,640]{2,1,0:T(8,128)(2,1)S(1)} async-done(((bf16[8,56,640]{2,1,0:T(8,128)(2,1)}), bf16[8,56,640]{2,1,0:T(8,128)(2,1)S(1)}, u32[]{:S(2)}, u32[]{:S(2)}) %all-to-all-start.7) | async-done | bytes 573472 | tf_op jit(solution)/shard_map/all_to_all | solution.py:32
  (57 shorter events, 7.5 us)
Async XLA Ops:
  7.2 51.3 %copy-start = (bf16[512,2048]{1,0:T(8,128)(2,1)S(1)}, bf16[512,2048]{1,0:T(8,128)(2,1)}, u32[]{:S(2)}) copy-start(bf16[512,2048]{1,0:T(8,128)(2,1)} %param.10) | copy-start | bytes 6291460
  8.9 16.9 %all-to-all-start.1 = ((bf16[4,16,2048]{2,1,0:T(8,128)(2,1)}), bf16[4,16,2048]{2,1,0:T(8,128)(2,1)S(1)}, u32[]{:S(2)}, u32[]{:S(2)}) async-start(bf16[4,16,2048]{2,1,0:T(8,128)(2,1)} %broadcast_in_dim.12), calls=%async_computation.1 | async-start | bytes 524288 | tf_op jit(solution)/shard_map/all_to_all | solution.py:32
  25.8 5.4 %copy-start.1 = (bf16[4,16,2048]{2,1,0:T(8,128)(2,1)}, bf16[4,16,2048]{2,1,0:T(8,128)(2,1)S(1)}, u32[]{:S(2)}) copy-start(bf16[4,16,2048]{2,1,0:T(8,128)(2,1)S(1)} %all-to-all-done.1) | copy-start | bytes 786436
  25.8 19.2 %copy-start.5 = (f32[512]{0:T(512)S(1)}, f32[512]{0:T(512)}, u32[]{:S(2)}) copy-start(f32[512]{0:T(512)} %param.8) | copy-start | bytes 6148
  25.8 19.0 %all-to-all-start = ((f32[16,32,512]{2,1,0:T(8,128)}), f32[16,32,512]{2,1,0:T(8,128)S(1)}, u32[]{:S(2)}, u32[]{:S(2)}) async-start(f32[16,32,512]{2,1,0:T(8,128)} %bitcast.28), calls=%async_computation | async-start | bytes 2097152 | tf_op jit(solution)/shard_map/all_to_all | solution.py:26
  31.1 45.9 %all-gather.2.cloned.1.call-start = ((), (), s32[]{:S(2)}) async-start(), calls=%async_computation.9 | async-start | bytes 2359296 | tf_op jit(solution)/shard_map/all_gather | solution.py:56
  80.6 17.9 %all-to-all-start.3 = ((bf16[16,32,512]{2,1,0:T(8,128)(2,1)}), bf16[16,32,512]{2,1,0:T(8,128)(2,1)S(1)}, u32[]{:S(2)}, u32[]{:S(2)}) async-start(bf16[16,32,512]{2,1,0:T(8,128)(2,1)} %bitcast.4), calls=%async_computation.3 | async-start | bytes 1048576 | tf_op jit(solution)/shard_map/all_to_all | solution.py:26
  90.8 49.9 %reduce-scatter.2.cloned.1.call-start = ((), (), s32[]{:S(2)}) async-start(), calls=%async_computation.10 | async-start | bytes 2359296 | tf_op jit(solution)/shard_map/reduce_scatter | solution.py:62
  98.6 8.0 %copy-start.4 = (bf16[512,64]{0,1:T(8,128)(2,1)S(1)}, bf16[512,64]{0,1:T(8,128)(2,1)}, u32[]{:S(2)}) copy-start(bf16[512,64]{0,1:T(8,128)(2,1)} %param.11) | copy-start | bytes 196612
  99.8 17.3 %copy-start.3 = (bf16[512,448]{0,1:T(8,128)(2,1)S(1)}, bf16[512,448]{0,1:T(8,128)(2,1)}, u32[]{:S(2)}) copy-start(bf16[512,448]{0,1:T(8,128)(2,1)} %param.6) | copy-start | bytes 1376260
  99.8 16.3 %all-to-all-start.4 = ((bf16[16,40,512]{2,1,0:T(8,128)(2,1)}), bf16[16,40,512]{2,1,0:T(8,128)(2,1)S(1)}, u32[]{:S(2)}, u32[]{:S(2)}) async-start(bf16[16,40,512]{2,1,0:T(8,128)(2,1)} %broadcast_in_dim.15), calls=%async_computation.4 | async-start | bytes 1310720 | tf_op jit(solution)/shard_map/all_to_all | solution.py:32
  116.3 0.8 copy-start.2
  118.6 26.3 %all-to-all-start.5 = ((bf16[8,56,640]{2,1,0:T(8,128)(2,1)}), bf16[8,56,640]{2,1,0:T(8,128)(2,1)S(1)}, u32[]{:S(2)}, u32[]{:S(2)}) async-start(bf16[8,56,640]{2,1,0:T(8,128)(2,1)} %pad_maximum_fusion.1), calls=%async_computation.5 | async-start | bytes 1146880 | tf_op jit(solution)/shard_map/all_to_all | solution.py:85
  163.4 30.6 %all-to-all-start.7 = ((bf16[8,56,640]{2,1,0:T(8,128)(2,1)}), bf16[8,56,640]{2,1,0:T(8,128)(2,1)S(1)}, u32[]{:S(2)}, u32[]{:S(2)}) async-start(bf16[8,56,640]{2,1,0:T(8,128)(2,1)} %broadcast_in_dim.17), calls=%async_computation.8 | async-start | bytes 1146880 | tf_op jit(solution)/shard_map/all_to_all | solution.py:32
Sparse Core Ops, SparseCore 0:
  34.6 42.3 all-gather.1
  94.4 46.1 reduce-scatter.1
where the time goes:
time: 203 us; the launch traced here: 202 us
  waiting for transfers between devices  91.1 us (45%)
  starting transfers between devices  44.6 us (22%)
  blocking collectives  30.4 us (15%)
  between operations  14.2 us (7%)
  matrix products  12 us (6%)
  local copies, waits for them, and re-layouts  7.94 us (4%)
  other arithmetic  2.25 us (1%)
    all_to_all x3, waiting for transfers between devices, spread(): return lax.all_to_all(copies, axes, 0, 0, tiled=True)  32.6 us
    all_to_all x3, starting transfers between devices, spread(): return lax.all_to_all(copies, axes, 0, 0, tiled=True)  25.3 us
    all_to_all x2, waiting for transfers between devices, scatter_sum(): arrived = lax.all_to_all(pieces, axes, 0, 0, tiled=True)  19.9 us
    reduce_scatter x1, waiting for transfers between devices, body(): up_sum = lax.psum_scatter(up_part, 'z', scatter_dimension=0, tiled=True)  18.2 us
    all_to_all x1, blocking collectives, body(): arrived = lax.all_to_all(both, 'yh', 0, 0, tiled=True)  17.1 us
    all_gather x1, waiting for transfers between devices, body(): w_up_all = lax.all_gather(w_up_near, 'z', axis=0, tiled=True)  15.9 us
    all_to_all x2, starting transfers between devices, scatter_sum(): arrived = lax.all_to_all(pieces, axes, 0, 0, tiled=True)  15.4 us
    all_to_all x1, blocking collectives, spread(): return lax.all_to_all(copies, axes, 0, 0, tiled=True)  13.3 us
  transfers between devices with their start and end apart: 8, of which 8 were waited for; matrix products, arithmetic and copies ran while one was open for 6% of the time, Pallas kernels for 0%

commit v1 on v0

--- a/solution.py
+++ b/solution.py
@@ -53,7 +53,10 @@
     lat = norm_gain.shape[0]
     width = w_down.shape[1]
     w_up_near = spread(w_up, "yh", n_yh).reshape(-1, w_up.shape[1])
-    w_up_all = lax.all_gather(w_up_near, "z", axis=0, tiled=True)
+    vals = []
+    for _ in range(lax.axis_size("z")):
+        vals.append(w_up_near)
+    w_up_all = jnp.concatenate(lax.all_to_all(jnp.stack(vals), "z", 0, 0), 0)
     projected = scatter_sum(dot(hidden, w_down[:, :lat], ((1,), (0,))), TENSOR, n_t)
     inv_rms = lax.rsqrt(jnp.mean(projected * projected, axis=1, keepdims=True) + 1e-06)
     latent = (projected * inv_rms * norm_gain).astype(jnp.bfloat16)

time: 203 us -> 240 us (1.18)
  the two profiles are of different devices: /device:TPU:23 before, /device:TPU:17 now
where the time goes in v1:
time: 240 us; the launch traced here: 239 us
  waiting for transfers between devices  108 us (45%)
  blocking collectives  63.3 us (26%)
  starting transfers between devices  32.1 us (13%)
  between operations  14.2 us (6%)
  matrix products  11.1 us (5%)
  local copies, waits for them, and re-layouts  8.53 us (4%)
    all_to_all x1, waiting for transfers between devices, body(): w_up_all = jnp.concatenate(lax.all_to_all(jnp.stack(vals), 'z', 0, 0), 0)  48.8 us
    all_to_all x3, waiting for transfers between devices, spread(): return lax.all_to_all(copies, axes, 0, 0, tiled=True)  32.6 us
    all_to_all x1, blocking collectives, body(): arrived = lax.all_to_all(both, 'yh', 0, 0, tiled=True)  25 us
    all_to_all x1, blocking collectives, scatter_sum(): arrived = lax.all_to_all(pieces, axes, 0, 0, tiled=True)  21.3 us
    all_to_all x1, blocking collectives, spread(): return lax.all_to_all(copies, axes, 0, 0, tiled=True)  16.9 us
    all_to_all x3, starting transfers between devices, spread(): return lax.all_to_all(copies, axes, 0, 0, tiled=True)  14.4 us
    dot_general x5, matrix products, dot(): lax.dot_general(a, b, (dims, ((), ())), preferred_element_type=jnp.float32)  11.1 us
    all_to_all x1, waiting for transfers between devices, body(): arrived = lax.all_to_all(packed, 'z', 0, 0, tiled=True).astype(jnp.float32)  10.1 us
  transfers between devices with their start and end apart: 7, of which 7 were waited for; matrix products, arithmetic and copies ran while one was open for 4% of the time, Pallas kernels for 0%

profile of v1, /device:TPU:17, one launch (start us, length us, event | category | flops | bytes accessed | tf_op | source)
XLA Modules:
  0.0 239.2 jit_solution(6658999956530890991)
XLA Ops:
  7.2 1.8 fusion.2
  9.0 21.3 %all_to_all.45 = f32[16,32,512]{2,1,0:T(8,128)S(1)} all-to-all(f32[16,32,512]{2,1,0:T(8,128)S(1)} %bitcast.29), channel_id=1, replica_groups=mesh['z'=8,'yh'=4,'x'=4,'yl'=2,'core'=2] {'x','yl','core'}, dimensions={0} | all-to-all | bytes 2097152 | tf_op jit(solution)/shard_map/all_to_all | solution.py:26
  31.0 6.2 %all-to-all-start.1 = ((bf16[4,16,2048]{2,1,0:T(8,128)(2,1)}), bf16[4,16,2048]{2,1,0:T(8,128)(2,1)S(1)}, u32[]{:S(2)}, u32[]{:S(2)}) async-start(bf16[4,16,2048]{2,1,0:T(8,128)(2,1)} %broadcast_in_dim.12), calls=%async_computation.1 | async-start | bytes 524288 | tf_op jit(solution)/shard_map/all_to_all | solution.py:32
  37.5 5.7 %all-to-all-done.1 = bf16[4,16,2048]{2,1,0:T(8,128)(2,1)S(1)} async-done(((bf16[4,16,2048]{2,1,0:T(8,128)(2,1)}), bf16[4,16,2048]{2,1,0:T(8,128)(2,1)S(1)}, u32[]{:S(2)}, u32[]{:S(2)}) %all-to-all-start.1) | async-done | bytes 262176 | tf_op jit(solution)/shard_map/all_to_all | solution.py:32
  43.3 16.9 %all_to_all.46 = bf16[16,32,512]{2,1,0:T(8,128)(2,1)S(1)} all-to-all(bf16[16,32,512]{2,1,0:T(8,128)(2,1)S(1)} %broadcast_in_dim.13), channel_id=1, replica_groups=mesh['z'=8,'yh'=4,'x'=4,'yl'=2,'core'=2] {'x','yl','core'}, dimensions={0} | all-to-all | bytes 1048576 | tf_op jit(solution)/shard_map/all_to_all | solution.py:32
  60.3 1.6 stack.8
  61.8 9.8 %all-to-all-start.2 = ((bf16[8,64,2048]{2,1,0:T(8,128)(2,1)}), bf16[8,64,2048]{2,1,0:T(8,128)(2,1)}, u32[]{:S(2)}, u32[]{:S(2)}) async-start(bf16[8,64,2048]{2,1,0:T(8,128)(2,1)} %stack.8), calls=%async_computation.2 | async-start | bytes 4194304 | tf_op jit(solution)/shard_map/all_to_all | solution.py:59
  71.6 2.6 %convolution_convert_fusion = bf16[512,2048]{1,0:T(8,128)(2,1)} fusion(bf16[512,512]{1,0:T(8,128)(2,1)S(1)} %bitcast.36, bf16[512,2048]{1,0:T(8,128)(2,1)S(1)} %copy-done), kind=kOutput, calls=%fused_computation | convolution fusion | flops 1074790400 | bytes 4718592 | tf_op jit(solution)/shard_map/dot_general | solution.py:15
  74.3 48.8 %all-to-all-done.2 = bf16[8,64,2048]{2,1,0:T(8,128)(2,1)} async-done(((bf16[8,64,2048]{2,1,0:T(8,128)(2,1)}), bf16[8,64,2048]{2,1,0:T(8,128)(2,1)}, u32[]{:S(2)}, u32[]{:S(2)}) %all-to-all-start.2) | async-done | bytes 2097184 | tf_op jit(solution)/shard_map/all_to_all | solution.py:59
  123.0 3.7 %convolution_convert_fusion.2 = bf16[512,512]{0,1:T(8,128)(2,1)} fusion(bf16[512,2048]{1,0:T(8,128)(2,1)} %bitcast.2, bf16[512,2048]{1,0:T(8,128)(2,1)S(1)} %copy-done), kind=kOutput, calls=%fused_computation.2 | convolution fusion | flops 1074003968 | bytes 4718592 | tf_op jit(solution)/shard_map/dot_general | solution.py:15
  126.7 4.3 %all-to-all-start.4 = ((bf16[16,32,512]{2,1,0:T(8,128)(2,1)}), bf16[16,32,512]{2,1,0:T(8,128)(2,1)S(1)}, u32[]{:S(2)}, u32[]{:S(2)}) async-start(bf16[16,32,512]{2,1,0:T(8,128)(2,1)} %bitcast.5), calls=%async_computation.4 | async-start | bytes 1048576 | tf_op jit(solution)/shard_map/all_to_all | solution.py:26
  131.8 9.1 %all-to-all-done.4 = bf16[16,32,512]{2,1,0:T(8,128)(2,1)S(1)} async-done(((bf16[16,32,512]{2,1,0:T(8,128)(2,1)}), bf16[16,32,512]{2,1,0:T(8,128)(2,1)S(1)}, u32[]{:S(2)}, u32[]{:S(2)}) %all-to-all-start.4) | async-done | bytes 524320 | tf_op jit(solution)/shard_map/all_to_all | solution.py:26
  141.3 0.9 broadcast_in_dim.15
  142.2 4.7 %all-to-all-start.5 = ((bf16[16,40,512]{2,1,0:T(8,128)(2,1)}), bf16[16,40,512]{2,1,0:T(8,128)(2,1)S(1)}, u32[]{:S(2)}, u32[]{:S(2)}) async-start(bf16[16,40,512]{2,1,0:T(8,128)(2,1)} %broadcast_in_dim.15), calls=%async_computation.5 | async-start | bytes 1310720 | tf_op jit(solution)/shard_map/all_to_all | solution.py:32
  147.0 11.2 %all-to-all-done.5 = bf16[16,40,512]{2,1,0:T(8,128)(2,1)S(1)} async-done(((bf16[16,40,512]{2,1,0:T(8,128)(2,1)}), bf16[16,40,512]{2,1,0:T(8,128)(2,1)S(1)}, u32[]{:S(2)}, u32[]{:S(2)}) %all-to-all-start.5) | async-done | bytes 655392 | tf_op jit(solution)/shard_map/all_to_all | solution.py:32
  159.7 0.9 pad_maximum_fusion.1
  160.6 3.5 %all-to-all-start.6 = ((bf16[8,56,640]{2,1,0:T(8,128)(2,1)}), bf16[8,56,640]{2,1,0:T(8,128)(2,1)S(1)}, u32[]{:S(2)}, u32[]{:S(2)}) async-start(bf16[8,56,640]{2,1,0:T(8,128)(2,1)} %pad_maximum_fusion.1), calls=%async_computation.6 | async-start | bytes 1146880 | tf_op jit(solution)/shard_map/all_to_all | solution.py:88
  164.2 6.3 %reduce-scatter.2.cloned.1.call-done = bf16[64,2048]{1,0:T(8,128)(2,1)} async-done(((bf16[512,2048]{1,0:T(8,128)(2,1)}), bf16[64,2048]{1,0:T(8,128)(2,1)}) %reduce-scatter.2.cloned.1.call-update) | async-done | bytes 262160 | tf_op jit(solution)/shard_map/reduce_scatter | solution.py:65
  170.5 1.1 reshape.146
  171.7 10.1 %all-to-all-done.6 = bf16[8,56,640]{2,1,0:T(8,128)(2,1)S(1)} async-done(((bf16[8,56,640]{2,1,0:T(8,128)(2,1)}), bf16[8,56,640]{2,1,0:T(8,128)(2,1)S(1)}, u32[]{:S(2)}, u32[]{:S(2)}) %all-to-all-start.6) | async-done | bytes 573472 | tf_op jit(solution)/shard_map/all_to_all | solution.py:88
  182.2 25.0 %all_to_all.47 = bf16[4,120,640]{2,1,0:T(8,128)(2,1)S(1)} all-to-all(bf16[4,120,640]{2,1,0:T(8,128)(2,1)S(1)} %fusion.1), channel_id=1, replica_groups=mesh['z'=8,'yh'=4,'x'=4,'yl'=2,'core'=2] {'yh'}, dimensions={0} | all-to-all | bytes 1228800 | tf_op jit(solution)/shard_map/all_to_all | solution.py:98
  208.3 3.5 %all-to-all-start.8 = ((bf16[8,56,640]{2,1,0:T(8,128)(2,1)}), bf16[8,56,640]{2,1,0:T(8,128)(2,1)S(1)}, u32[]{:S(2)}, u32[]{:S(2)}) async-start(bf16[8,56,640]{2,1,0:T(8,128)(2,1)} %broadcast_in_dim.17), calls=%async_computation.9 | async-start | bytes 1146880 | tf_op jit(solution)/shard_map/all_to_all | solution.py:32
  211.8 2.5 %convolution_convert_fusion.3 = bf16[512,448]{0,1:T(8,128)(2,1)} fusion(bf16[448,576]{1,0:T(8,128)(2,1)} %param.7, bf16[512,64]{1,0:T(8,128)(2,1)S(1)} %copy.27, bf16[512,512]{1,0:T(8,128)(2,1)} %bitcast.35), kind=kOutput, calls=%fused_computation.3 | convolution fusion | flops 265650176 | bytes 1564672 | tf_op jit(solution)/shard_map/dot_general | solution.py:15
  215.0 15.7 %all-to-all-done.8 = bf16[8,56,640]{2,1,0:T(8,128)(2,1)S(1)} async-done(((bf16[8,56,640]{2,1,0:T(8,128)(2,1)}), bf16[8,56,640]{2,1,0:T(8,128)(2,1)S(1)}, u32[]{:S(2)}, u32[]{:S(2)}) %all-to-all-start.8) | async-done | bytes 573472 | tf_op jit(solution)/shard_map/all_to_all | solution.py:32
  (56 shorter events, 7.5 us)
Async XLA Ops:
  7.2 64.5 %copy-start = (bf16[512,2048]{1,0:T(8,128)(2,1)S(1)}, bf16[512,2048]{1,0:T(8,128)(2,1)}, u32[]{:S(2)}) copy-start(bf16[512,2048]{1,0:T(8,128)(2,1)} %param.10) | copy-start | bytes 6291460
  9.0 21.4 %copy-start.3 = (bf16[16,2048]{1,0:T(8,128)(2,1)S(1)}, bf16[16,2048]{1,0:T(8,128)(2,1)}, u32[]{:S(2)}) copy-start(bf16[16,2048]{1,0:T(8,128)(2,1)} %param.9) | copy-start | bytes 196612
  30.3 7.1 %copy-start.5 = (f32[512]{0:T(512)S(1)}, f32[512]{0:T(512)}, u32[]{:S(2)}) copy-start(f32[512]{0:T(512)} %param.8) | copy-start | bytes 6148
  31.0 12.2 %all-to-all-start.1 = ((bf16[4,16,2048]{2,1,0:T(8,128)(2,1)}), bf16[4,16,2048]{2,1,0:T(8,128)(2,1)S(1)}, u32[]{:S(2)}, u32[]{:S(2)}) async-start(bf16[4,16,2048]{2,1,0:T(8,128)(2,1)} %broadcast_in_dim.12), calls=%async_computation.1 | async-start | bytes 524288 | tf_op jit(solution)/shard_map/all_to_all | solution.py:32
  61.8 61.2 %all-to-all-start.2 = ((bf16[8,64,2048]{2,1,0:T(8,128)(2,1)}), bf16[8,64,2048]{2,1,0:T(8,128)(2,1)}, u32[]{:S(2)}, u32[]{:S(2)}) async-start(bf16[8,64,2048]{2,1,0:T(8,128)(2,1)} %stack.8), calls=%async_computation.2 | async-start | bytes 4194304 | tf_op jit(solution)/shard_map/all_to_all | solution.py:59
  126.7 14.2 %all-to-all-start.4 = ((bf16[16,32,512]{2,1,0:T(8,128)(2,1)}), bf16[16,32,512]{2,1,0:T(8,128)(2,1)S(1)}, u32[]{:S(2)}, u32[]{:S(2)}) async-start(bf16[16,32,512]{2,1,0:T(8,128)(2,1)} %bitcast.5), calls=%async_computation.4 | async-start | bytes 1048576 | tf_op jit(solution)/shard_map/all_to_all | solution.py:26
  131.0 39.5 %reduce-scatter.2.cloned.1.call-start = ((), (), s32[]{:S(2)}) async-start(), calls=%async_computation.10 | async-start | bytes 2359296 | tf_op jit(solution)/shard_map/reduce_scatter | solution.py:65
  141.0 5.9 %copy-start.4 = (bf16[512,64]{0,1:T(8,128)(2,1)S(1)}, bf16[512,64]{0,1:T(8,128)(2,1)}, u32[]{:S(2)}) copy-start(bf16[512,64]{0,1:T(8,128)(2,1)} %param.11) | copy-start | bytes 196612
  142.2 17.0 %copy-start.2 = (bf16[512,448]{0,1:T(8,128)(2,1)S(1)}, bf16[512,448]{0,1:T(8,128)(2,1)}, u32[]{:S(2)}) copy-start(bf16[512,448]{0,1:T(8,128)(2,1)} %param.6) | copy-start | bytes 1376260
  142.2 16.0 %all-to-all-start.5 = ((bf16[16,40,512]{2,1,0:T(8,128)(2,1)}), bf16[16,40,512]{2,1,0:T(8,128)(2,1)S(1)}, u32[]{:S(2)}, u32[]{:S(2)}) async-start(bf16[16,40,512]{2,1,0:T(8,128)(2,1)} %broadcast_in_dim.15), calls=%async_computation.5 | async-start | bytes 1310720 | tf_op jit(solution)/shard_map/all_to_all | solution.py:32
  158.4 0.8 copy-start.1
  160.6 21.1 %all-to-all-start.6 = ((bf16[8,56,640]{2,1,0:T(8,128)(2,1)}), bf16[8,56,640]{2,1,0:T(8,128)(2,1)S(1)}, u32[]{:S(2)}, u32[]{:S(2)}) async-start(bf16[8,56,640]{2,1,0:T(8,128)(2,1)} %pad_maximum_fusion.1), calls=%async_computation.6 | async-start | bytes 1146880 | tf_op jit(solution)/shard_map/all_to_all | solution.py:88
  208.3 22.5 %all-to-all-start.8 = ((bf16[8,56,640]{2,1,0:T(8,128)(2,1)}), bf16[8,56,640]{2,1,0:T(8,128)(2,1)S(1)}, u32[]{:S(2)}, u32[]{:S(2)}) async-start(bf16[8,56,640]{2,1,0:T(8,128)(2,1)} %broadcast_in_dim.17), calls=%async_computation.9 | async-start | bytes 1146880 | tf_op jit(solution)/shard_map/all_to_all | solution.py:32
Sparse Core Ops, SparseCore 0:
  134.7 35.7 reduce-scatter.1
